TPU v7x, 32 devices: a whole 2x2x4 slice. The times are simulated.
32 devices in a mesh: gx: 4 (over y, x), gy: 2 (over core), gz: 4 (over z).
Axes of the slice: x: 2, y: 2, z: 4, core: 2. Of those that a mesh axis runs over, the one named last changes fastest.
Arguments:
- thermal_field: float32 [32, 32, 512], P('gz', 'gy', 'gx'), may hold values from -2 to 4
- forcing_per_step: float32 [32, 32, 512], P('gz', 'gy', 'gx'), may hold values from 0.1 to 4
- substance_label: int32 [32, 32, 512], P('gz', 'gy', 'gx'), may hold values from 0 to 7
- thermal_conductivities: float32 [8], replicated, may hold values from 0.5 to 4
- patch_group_label: int32 [4, 4, 16], P('gz', 'gy', 'gx'), may hold values from 0 to 63, as said below
- drain_power_density: float32 [64], replicated, may hold values from 0.2 to 2
Outputs:
- next_thermal_field: float32 [32, 32, 512], P('gz', 'gy', 'gx')
- forcing_with_drain: float32 [32, 32, 512], P('gz', 'gy', 'gx')
Inputs may be any that keep to these rules, and one draw needn't show every extreme that they name: `patch_group_label`: every cluster labels exactly four tiles.
All inputs are finite; a program needn't handle non-finite values.
Results may differ from a plain program's by a relative error of at most 0.0003.
Values sent between devices are 32-bit elements; how exact they have to be, the bound alone decides.
A program may use at most 64 MiB of HBM per device.

v0:
```python
import jax
import jax.numpy as jnp
from jax import lax
from jax.sharding import PartitionSpec as P

TX = 32
TY = 8
IMPLICIT_WEIGHT = 0.5
LATERAL_RATE = 100.0
VERTICAL_RATE = 400.0
SOURCE_STEP = 0.5
LEAK_SLOPE = 0.5


def padded(shard, sides, width):
    for axis, dim in sides:
        devices, length = (lax.axis_size(axis), shard.shape[dim])
        up = [(i, (i + 1) % devices) for i in range(devices - 1)]
        down = [(j, i) for i, j in up]
        last = lax.slice_in_dim(shard, length - width, length, axis=dim)
        first = lax.slice_in_dim(shard, 0, width, axis=dim)
        before = lax.ppermute(last, axis, up)
        after = lax.ppermute(first, axis, down)
        shard = jnp.concatenate([before, shard, after], axis=dim)
    return shard


def harmonic(first_k, second_k):
    return 2.0 * first_k * second_k / (first_k + second_k)


def chain_solve(gathered, position):
    zero_line = jnp.zeros_like(gathered[0, 0])

    def forward(state_pair, column):
        carry_const, carry_slope = state_pair
        divisor = 1.0 - carry_slope * column[2]
        offset = (column[0] - column[2] * carry_const) / divisor
        slope = -column[4] / divisor
        next_const = column[1] - column[3] * (carry_const - carry_slope * column[0]) / divisor
        next_slope = column[5] + column[3] * carry_slope * column[4] / divisor
        return ((next_const, next_slope), (carry_const, carry_slope, offset, slope))

    _, (consts, slopes, offsets, gradients) = lax.scan(forward, (zero_line, zero_line), gathered)

    def backward(next_value, item):
        offset, slope, carry_const, carry_slope = item
        value = offset + slope * next_value
        return (value, (next_value, carry_const - carry_slope * value))

    _, (right_values, left_values) = lax.scan(
        backward, zero_line, (offsets, gradients, consts, slopes), reverse=True
    )
    left_value = lax.dynamic_index_in_dim(left_values, position, 0, keepdims=False)
    right_value = lax.dynamic_index_in_dim(right_values, position, 0, keepdims=False)
    return (left_value, right_value)


def interface_x(coeffs):
    gathered = lax.all_gather(coeffs[None], "gx", axis=0, tiled=True)
    return chain_solve(gathered, lax.axis_index("gx"))


def interface_y(coeffs):
    gathered = lax.all_gather(coeffs[None], "gy", axis=0, tiled=True)
    return chain_solve(gathered, lax.axis_index("gy"))


def interface_z(coeffs):
    gathered = lax.all_gather(coeffs[None], "gz", axis=0, tiled=True)
    return chain_solve(gathered, lax.axis_index("gz"))


def shifted(values, offset, axis, filler):
    length = values.shape[axis]
    pad_shape = list(values.shape)
    pad_shape[axis] = abs(offset)
    padding = jnp.full(tuple(pad_shape), filler, values.dtype)
    if offset > 0:
        return jnp.concatenate(
            [padding, lax.slice_in_dim(values, 0, length - offset, axis=axis)], axis=axis
        )
    return jnp.concatenate(
        [lax.slice_in_dim(values, -offset, length, axis=axis), padding], axis=axis
    )


def reduce_lines(right_side, face, axis, interface):
    length = right_side.shape[axis]
    low_face = lax.slice_in_dim(face, 0, length, axis=axis)
    high_face = lax.slice_in_dim(face, 1, length + 1, axis=axis)
    places = lax.broadcasted_iota(jnp.int32, right_side.shape, axis)
    lower_band = -IMPLICIT_WEIGHT * low_face
    upper_band = -IMPLICIT_WEIGHT * high_face
    main_band = 1.0 + IMPLICIT_WEIGHT * (low_face + high_face)
    left_side = jnp.where(places == 0, lower_band, 0.0)
    right_edge = jnp.where(places == length - 1, upper_band, 0.0)
    sub_band = jnp.where(places == 0, 0.0, lower_band)
    super_band = jnp.where(places == length - 1, 0.0, upper_band)
    sources = [right_side, left_side, right_edge]
    stride = 1
    while stride < length:
        sub_down = shifted(sub_band, stride, axis, 0.0)
        main_down = shifted(main_band, stride, axis, 1.0)
        super_down = shifted(super_band, stride, axis, 0.0)
        sub_up = shifted(sub_band, -stride, axis, 0.0)
        main_up = shifted(main_band, -stride, axis, 1.0)
        super_up = shifted(super_band, -stride, axis, 0.0)
        factor_down = -sub_band / main_down
        factor_up = -super_band / main_up
        sources = [
            source
            + factor_down * shifted(source, stride, axis, 0.0)
            + factor_up * shifted(source, -stride, axis, 0.0)
            for source in sources
        ]
        main_band = main_band + factor_down * super_down + factor_up * sub_up
        sub_band = factor_down * sub_down
        super_band = factor_up * super_up
        stride = stride * 2
    local_part, left_part, right_part = [source / main_band for source in sources]
    coeffs = jnp.stack(
        [
            lax.index_in_dim(local_part, 0, axis, keepdims=False),
            lax.index_in_dim(local_part, length - 1, axis, keepdims=False),
            lax.index_in_dim(left_part, 0, axis, keepdims=False),
            lax.index_in_dim(left_part, length - 1, axis, keepdims=False),
            lax.index_in_dim(right_part, 0, axis, keepdims=False),
            lax.index_in_dim(right_part, length - 1, axis, keepdims=False),
        ]
    )
    left_value, right_value = interface(coeffs)
    return (
        local_part
        - jnp.expand_dims(left_value, axis) * left_part
        - jnp.expand_dims(right_value, axis) * right_part
    )


def per_device(
    thermal_field,
    forcing_per_step,
    substance_label,
    thermal_conductivities,
    patch_group_label,
    drain_power_density,
):
    layer_voxel_number, height_voxel_number, width_voxel_number = thermal_field.shape
    voxel_thermal_link = jnp.zeros(thermal_field.shape, jnp.float32)
    for level in range(thermal_conductivities.shape[0]):
        voxel_thermal_link = voxel_thermal_link + jnp.where(
            substance_label == level, thermal_conductivities[level], 0.0
        )
    joined_outputs = jnp.stack([thermal_field, voxel_thermal_link])
    bordered_array = padded(joined_outputs, (("gx", 3), ("gy", 2), ("gz", 1)), 1)
    bordered_thermal_field = bordered_array[0]
    padk = bordered_array[1]
    sideways_link_xaxis = LATERAL_RATE * harmonic(padk[1:-1, 1:-1, :-1], padk[1:-1, 1:-1, 1:])
    sideways_link_yaxis = LATERAL_RATE * harmonic(padk[1:-1, :-1, 1:-1], padk[1:-1, 1:, 1:-1])
    upward_link_strength = VERTICAL_RATE * harmonic(padk[:-1, 1:-1, 1:-1], padk[1:, 1:-1, 1:-1])
    energy_current = sideways_link_xaxis[:, :, 1:] * (
        bordered_thermal_field[1:-1, 1:-1, 2:] - thermal_field
    ) - sideways_link_xaxis[:, :, :-1] * (thermal_field - bordered_thermal_field[1:-1, 1:-1, :-2])
    energy_current = (
        energy_current
        + sideways_link_yaxis[:, 1:, :] * (bordered_thermal_field[1:-1, 2:, 1:-1] - thermal_field)
        - sideways_link_yaxis[:, :-1, :] * (thermal_field - bordered_thermal_field[1:-1, :-2, 1:-1])
    )
    energy_current = (
        energy_current
        + upward_link_strength[1:] * (bordered_thermal_field[2:, 1:-1, 1:-1] - thermal_field)
        - upward_link_strength[:-1] * (thermal_field - bordered_thermal_field[:-2, 1:-1, 1:-1])
    )
    residual = SOURCE_STEP * forcing_per_step + energy_current
    step_x = reduce_lines(residual, sideways_link_xaxis, 2, interface_x)
    step_y = reduce_lines(step_x, sideways_link_yaxis, 1, interface_y)
    upward_correction = reduce_lines(step_y, upward_link_strength, 0, interface_z)
    next_thermal_field = thermal_field + upward_correction
    patch_extents = (
        layer_voxel_number,
        height_voxel_number // TY,
        TY,
        width_voxel_number // TX,
        TX,
    )
    patch_power_sum = next_thermal_field.reshape(patch_extents).sum(axis=(0, 2, 4)).reshape(-1)
    local_labels = patch_group_label.reshape(-1)
    cluster_count = drain_power_density.shape[0]
    onehot = (local_labels[:, None] == jnp.arange(cluster_count)[None, :]).astype(jnp.float32)
    partial_value = jnp.dot(patch_power_sum, onehot, precision=lax.Precision.HIGHEST)
    cluster_cells = 4 * layer_voxel_number * TY * TX
    cluster_total = lax.psum(partial_value, ("gx", "gy", "gz"))
    leak_power = drain_power_density * jnp.exp(LEAK_SLOPE * (cluster_total / cluster_cells))
    tile_power = jnp.dot(onehot, leak_power, precision=lax.Precision.HIGHEST)
    forcing_with_drain = forcing_per_step.reshape(patch_extents) + tile_power.reshape(
        1, height_voxel_number // TY, 1, width_voxel_number // TX, 1
    )
    return (next_thermal_field, forcing_with_drain.reshape(forcing_per_step.shape))


def solution(mesh):
    in_specs = (
        P("gz", "gy", "gx"),
        P("gz", "gy", "gx"),
        P("gz", "gy", "gx"),
        P(),
        P("gz", "gy", "gx"),
        P(),
    )
    out_specs = (P("gz", "gy", "gx"), P("gz", "gy", "gx"))
    return jax.shard_map(
        per_device, mesh=mesh, in_specs=in_specs, out_specs=out_specs, check_vma=False
    )
```

profile of v0, /device:TPU:0, one launch (start us, length us, event | category | flops | bytes accessed | tf_op | source)
XLA Modules:
  0.0 110.0 jit_solution(4359483157431193662)
XLA Ops:
  0.6 1.6 %fusion.115 = (f32[1]{0:T(128)}, f32[1]{0:T(128)}, f32[1]{0:T(128)}, f32[1]{0:T(128)}, f32[1]{0:T(128)}, /*index=5*/f32[1]{0:T(128)}, f32[1]{0:T(128)}, f32[1]{0:T(128)}) fusion(f32[8]{0:T(128)} %param.21), kind=kLoop, calls=%fused_computation.347 | loop fusion | bytes 64 | tf_op jit(solution)/shard_map/slice | solution.py:152
  2.3 5.9 %add_bitcast_fusion = f32[1,8,16,128]{3,2,1,0:T(8,128)S(1)} fusion(s32[8,16,128]{2,1,0:T(8,128)} %param.20, f32[]{:T(128)} %bitcast.8, f32[]{:T(128)} %bitcast.7, f32[]{:T(128)} %bitcast.6, f32[]{:T(128)} %bitcast.5, f32[]{:T(128)} %bitcast.4, f32[]{:T(128)} %bitcast.3, f32[]{:T(128)} %bitcast.2, f32[]{:T(128)} %bitcast.1), kind=kLoop, calls=%fused_computation.203 | loop fusion | flops 376832 | bytes 131104 | tf_op jit(solution)/shard_map/stack | solution.py:154
  8.3 4.8 %collective-permute-start = (f32[2,8,16,1]{3,2,1,0:T(8,128)S(1)}, f32[2,8,16,1]{3,2,1,0:T(8,128)S(1)}, u32[]{:S(2)}, u32[]{:S(2)}) collective-permute-start(f32[2,8,16,1]{3,2,1,0:T(8,128)S(1)} %get-tuple-element.1143), channel_id=1, source_target_pairs={{0,8},{8,16},{16,24},{1,9},{9,17},{17,25},{2,10},{10,18},{18,26},{... | collective-permute-start | bytes 3080 | tf_op jit(solution)/shard_map/ppermute | solution.py:22
  13.2 1.3 %collective-permute-start.1 = (f32[2,8,16,1]{3,2,1,0:T(8,128)S(1)}, f32[2,8,16,1]{3,2,1,0:T(8,128)S(1)}, u32[]{:S(2)}, u32[]{:S(2)}) collective-permute-start(f32[2,8,16,1]{3,2,1,0:T(8,128)S(1)} %get-tuple-element.1144), channel_id=1, source_target_pairs={{8,0},{16,8},{24,16},{9,1},{17,9},{25,17},{10,2},{18,10},{26,18},{... | collective-permute-start | bytes 3080 | tf_op jit(solution)/shard_map/ppermute | solution.py:23
  14.5 1.4 %collective-permute-done = f32[2,8,16,1]{3,2,1,0:T(8,128)S(1)} collective-permute-done((f32[2,8,16,1]{3,2,1,0:T(8,128)S(1)}, f32[2,8,16,1]{3,2,1,0:T(8,128)S(1)}, u32[]{:S(2)}, u32[]{:S(2)}) %collective-permute-start) | collective-permute-done | bytes 1056 | tf_op jit(solution)/shard_map/ppermute | solution.py:22
  15.9 4.8 %collective-permute-done.1 = f32[2,8,16,1]{3,2,1,0:T(8,128)S(1)} collective-permute-done((f32[2,8,16,1]{3,2,1,0:T(8,128)S(1)}, f32[2,8,16,1]{3,2,1,0:T(8,128)S(1)}, u32[]{:S(2)}, u32[]{:S(2)}) %collective-permute-start.1) | collective-permute-done | bytes 1056 | tf_op jit(solution)/shard_map/ppermute | solution.py:23
  20.7 0.2 pad_maximum_fusion.11
  20.8 1.3 %collective-permute-start.2 = (f32[2,8,1,130]{3,1,2,0:T(8,128)S(1)}, f32[2,8,1,130]{3,1,2,0:T(8,128)S(1)}, u32[]{:S(2)}, u32[]{:S(2)}) collective-permute-start(f32[2,8,1,130]{3,1,2,0:T(8,128)S(1)} %copy.710), channel_id=1, source_target_pairs={{0,4},{1,5},{2,6},{3,7},{8,12},{9,13},{10,14},{11,15},{16,20},{17,... | collective-permute-start | bytes 24968 | tf_op jit(solution)/shard_map/ppermute | solution.py:22
  22.2 1.3 %collective-permute-start.3 = (f32[2,8,1,130]{3,1,2,0:T(8,128)S(1)}, f32[2,8,1,130]{3,1,2,0:T(8,128)S(1)}, u32[]{:S(2)}, u32[]{:S(2)}) collective-permute-start(f32[2,8,1,130]{3,1,2,0:T(8,128)S(1)} %copy.711), channel_id=1, source_target_pairs={{4,0},{5,1},{6,2},{7,3},{12,8},{13,9},{14,10},{15,11},{20,16},{21,... | collective-permute-start | bytes 24968 | tf_op jit(solution)/shard_map/ppermute | solution.py:23
  23.5 1.7 %collective-permute-done.3 = f32[2,8,1,130]{3,1,2,0:T(8,128)S(1)} collective-permute-done((f32[2,8,1,130]{3,1,2,0:T(8,128)S(1)}, f32[2,8,1,130]{3,1,2,0:T(8,128)S(1)}, u32[]{:S(2)}, u32[]{:S(2)}) %collective-permute-start.3) | collective-permute-done | bytes 8352 | tf_op jit(solution)/shard_map/ppermute | solution.py:23
  25.4 3.5 %collective-permute-start.4 = (f32[2,1,18,130]{3,2,1,0:T(8,128)S(1)}, f32[2,1,18,130]{3,2,1,0:T(8,128)S(1)}, u32[]{:S(2)}, u32[]{:S(2)}) collective-permute-start(f32[2,1,18,130]{3,2,1,0:T(8,128)S(1)} %get-tuple-element.1066), channel_id=1, source_target_pairs={{0,1},{1,2},{2,3},{4,5},{5,6},{6,7},{8,9},{9,10},{10,11},{12,13},{... | collective-permute-start | bytes 56168 | tf_op jit(solution)/shard_map/ppermute | solution.py:22
  28.9 1.3 %collective-permute-start.5 = (f32[2,1,18,130]{3,2,1,0:T(8,128)S(1)}, f32[2,1,18,130]{3,2,1,0:T(8,128)S(1)}, u32[]{:S(2)}, u32[]{:S(2)}) collective-permute-start(f32[2,1,18,130]{3,2,1,0:T(8,128)S(1)} %get-tuple-element.1067), channel_id=1, source_target_pairs={{1,0},{2,1},{3,2},{5,4},{6,5},{7,6},{9,8},{10,9},{11,10},{13,12},{... | collective-permute-start | bytes 56168 | tf_op jit(solution)/shard_map/ppermute | solution.py:23
  30.3 0.7 copy-done.2
  31.0 3.8 %collective-permute-done.5 = f32[2,1,18,130]{3,2,1,0:T(8,128)S(1)} collective-permute-done((f32[2,1,18,130]{3,2,1,0:T(8,128)S(1)}, f32[2,1,18,130]{3,2,1,0:T(8,128)S(1)}, u32[]{:S(2)}, u32[]{:S(2)}) %collective-permute-start.5) | collective-permute-done | bytes 18752 | tf_op jit(solution)/shard_map/ppermute | solution.py:23
  34.8 0.2 pad_maximum_fusion
  35.8 0.8 copy-done.1
  36.6 0.2 fusion.14
  37.6 0.2 multiply_add_fusion.48
  38.4 0.2 multiply_add_fusion.46
  39.2 0.2 multiply_add_fusion.44
  40.0 0.2 multiply_add_fusion.42
  40.8 0.2 multiply_add_fusion.40
  42.7 8.6 %all-gather = f32[24,8,16]{2,1,0:T(8,128)S(1)} all-gather(f32[6,8,16]{2,1,0:T(8,128)S(1)} %constant_dynamic-update-slice_fusion), channel_id=2, replica_groups=mesh['gx'=4,'gy'=2,'gz'=4] {'gx'}, dimensions={0}, use_global_device_ids=true | all-gather | bytes 15360 | tf_op jit(solution)/shard_map/all_gather | solution.py:60
  51.4 0.3 while.120
  52.9 1.8 %all-gather.1 = f32[12,8,128]{2,1,0:T(8,128)S(1)} all-gather(f32[6,8,128]{2,1,0:T(8,128)S(1)} %constant_dynamic-update-slice_fusion.6), channel_id=3, replica_groups=mesh['gx'=4,'gy'=2,'gz'=4] {'gy'}, dimensions={0}, use_global_device_ids=true | all-gather | bytes 73728 | tf_op jit(solution)/shard_map/all_gather | solution.py:65
  55.9 13.8 %all-gather.2 = f32[24,16,128]{2,1,0:T(8,128)S(1)} all-gather(f32[6,16,128]{2,1,0:T(8,128)S(1)} %constant_dynamic-update-slice_fusion.12), channel_id=4, replica_groups=mesh['gx'=4,'gy'=2,'gz'=4] {'gz'}, dimensions={0}, use_global_device_ids=true | all-gather | bytes 245760 | tf_op jit(solution)/shard_map/all_gather | solution.py:70
  69.7 0.3 while.124
  70.3 0.7 fusion.33
  71.2 0.2 convolution_bitcast_fusion.1
  71.4 37.5 %psum.7 = f32[64]{0:T(128)S(1)} all-reduce(f32[64]{0:T(128)S(1)} %convolution_bitcast_fusion.1), channel_id=1, replica_groups=mesh['gx'=4,'gy'=2,'gz'=4] {'gx','gy','gz'}, use_global_device_ids=true, to_apply=%region_14.15 | all-reduce | flops 64 | bytes 512 | tf_op jit(solution)/shard_map/psum | solution.py:192
  108.9 0.2 convolution_bitcast_fusion
  109.3 0.6 broadcast_add_fusion
  (229 shorter events, 9.1 us)
Async XLA Ops:
  2.3 5.9 %copy-start = (f32[8,16,128]{2,1,0:T(8,128)S(1)}, f32[8,16,128]{2,1,0:T(8,128)}, u32[]{:S(2)}) copy-start(f32[8,16,128]{2,1,0:T(8,128)} %param.18) | copy-start | bytes 196612
  8.3 7.6 %collective-permute-start = (f32[2,8,16,1]{3,2,1,0:T(8,128)S(1)}, f32[2,8,16,1]{3,2,1,0:T(8,128)S(1)}, u32[]{:S(2)}, u32[]{:S(2)}) collective-permute-start(f32[2,8,16,1]{3,2,1,0:T(8,128)S(1)} %get-tuple-element.1143), channel_id=1, source_target_pairs={{0,8},{8,16},{16,24},{1,9},{9,17},{17,25},{2,10},{10,18},{18,26},{... | collective-permute-start | bytes 3080 | tf_op jit(solution)/shard_map/ppermute | solution.py:22
  13.2 7.5 %collective-permute-start.1 = (f32[2,8,16,1]{3,2,1,0:T(8,128)S(1)}, f32[2,8,16,1]{3,2,1,0:T(8,128)S(1)}, u32[]{:S(2)}, u32[]{:S(2)}) collective-permute-start(f32[2,8,16,1]{3,2,1,0:T(8,128)S(1)} %get-tuple-element.1144), channel_id=1, source_target_pairs={{8,0},{16,8},{24,16},{9,1},{17,9},{25,17},{10,2},{18,10},{26,18},{... | collective-permute-start | bytes 3080 | tf_op jit(solution)/shard_map/ppermute | solution.py:23
  20.8 2.6 %collective-permute-start.2 = (f32[2,8,1,130]{3,1,2,0:T(8,128)S(1)}, f32[2,8,1,130]{3,1,2,0:T(8,128)S(1)}, u32[]{:S(2)}, u32[]{:S(2)}) collective-permute-start(f32[2,8,1,130]{3,1,2,0:T(8,128)S(1)} %copy.710), channel_id=1, source_target_pairs={{0,4},{1,5},{2,6},{3,7},{8,12},{9,13},{10,14},{11,15},{16,20},{17,... | collective-permute-start | bytes 24968 | tf_op jit(solution)/shard_map/ppermute | solution.py:22
  22.2 3.1 %collective-permute-start.3 = (f32[2,8,1,130]{3,1,2,0:T(8,128)S(1)}, f32[2,8,1,130]{3,1,2,0:T(8,128)S(1)}, u32[]{:S(2)}, u32[]{:S(2)}) collective-permute-start(f32[2,8,1,130]{3,1,2,0:T(8,128)S(1)} %copy.711), channel_id=1, source_target_pairs={{4,0},{5,1},{6,2},{7,3},{12,8},{13,9},{14,10},{15,11},{20,16},{21,... | collective-permute-start | bytes 24968 | tf_op jit(solution)/shard_map/ppermute | solution.py:23
  25.4 5.7 %collective-permute-start.4 = (f32[2,1,18,130]{3,2,1,0:T(8,128)S(1)}, f32[2,1,18,130]{3,2,1,0:T(8,128)S(1)}, u32[]{:S(2)}, u32[]{:S(2)}) collective-permute-start(f32[2,1,18,130]{3,2,1,0:T(8,128)S(1)} %get-tuple-element.1066), channel_id=1, source_target_pairs={{0,1},{1,2},{2,3},{4,5},{5,6},{6,7},{8,9},{9,10},{10,11},{12,13},{... | collective-permute-start | bytes 56168 | tf_op jit(solution)/shard_map/ppermute | solution.py:22
  28.9 6.0 %collective-permute-start.5 = (f32[2,1,18,130]{3,2,1,0:T(8,128)S(1)}, f32[2,1,18,130]{3,2,1,0:T(8,128)S(1)}, u32[]{:S(2)}, u32[]{:S(2)}) collective-permute-start(f32[2,1,18,130]{3,2,1,0:T(8,128)S(1)} %get-tuple-element.1067), channel_id=1, source_target_pairs={{1,0},{2,1},{3,2},{5,4},{6,5},{7,6},{9,8},{10,9},{11,10},{13,12},{... | collective-permute-start | bytes 56168 | tf_op jit(solution)/shard_map/ppermute | solution.py:23
  30.3 0.7 copy-start.2
  35.8 0.8 copy-start.1
  71.4 37.5 %copy-start.3 = (f32[64]{0:T(128)S(1)}, f32[64]{0:T(128)}, u32[]{:S(2)}) copy-start(f32[64]{0:T(128)} %param.23) | copy-start | bytes 772
where the time goes:
time: 111 us; the launch traced here: 110 us
  blocking collectives  61.8 us (56%)
  starting transfers between devices  13.5 us (12%)
  other arithmetic  12.2 us (11%)
  waiting for transfers between devices  11.7 us (11%)
  local copies, waits for them, and re-layouts  8.1 us (7%)
  between operations  1.81 us (2%)
    psum x1, blocking collectives, per_device(): cluster_total = lax.psum(partial_value, ('gx', 'gy', 'gz'))  37.5 us
    all_gather x1, blocking collectives, interface_z(): gathered = lax.all_gather(coeffs[None], 'gz', axis=0, tiled=True)  13.8 us
    ppermute x3, waiting for transfers between devices, padded(): after = lax.ppermute(first, axis, down)  10.3 us
    ppermute x3, starting transfers between devices, padded(): before = lax.ppermute(last, axis, up)  9.62 us
    all_gather x1, blocking collectives, interface_x(): gathered = lax.all_gather(coeffs[None], 'gx', axis=0, tiled=True)  8.61 us
    another operation x2, other arithmetic, per_device(): joined_outputs = jnp.stack([thermal_field, voxel_thermal_link])  6.03 us
    ppermute x3, starting transfers between devices, padded(): after = lax.ppermute(first, axis, down)  3.88 us
    slice x50, local copies, waits for them, and re-layouts, shifted(): lax.slice_in_dim(values, 0, length - offset, axis=axis)  2.41 us
  transfers between devices with their start and end apart: 6, of which 4 were waited for; matrix products, arithmetic and copies ran while one was open for 0% of the time, Pallas kernels for 0%

commit v1 on v0

--- a/solution.py
+++ b/solution.py
@@ -189,7 +189,7 @@
     onehot = (local_labels[:, None] == jnp.arange(cluster_count)[None, :]).astype(jnp.float32)
     partial_value = jnp.dot(patch_power_sum, onehot, precision=lax.Precision.HIGHEST)
     cluster_cells = 4 * layer_voxel_number * TY * TX
-    cluster_total = lax.psum(partial_value, ("gx", "gy", "gz"))
+    cluster_total = lax.psum(lax.psum(partial_value, ("gy", "gz")), "gx")
     leak_power = drain_power_density * jnp.exp(LEAK_SLOPE * (cluster_total / cluster_cells))
     tile_power = jnp.dot(onehot, leak_power, precision=lax.Precision.HIGHEST)
     forcing_with_drain = forcing_per_step.reshape(patch_extents) + tile_power.reshape(

time: 111 us -> 95.7 us (0.86)
  blocking collectives: 61.8 us -> 46.9 us
    psum x1 -> x2, blocking collectives: 37.5 us -> 22.6 us  [per_device(): cluster_total = lax.psum(lax.psum(partial_value, ('gy', 'gz')), 'gx')]
where the time goes in v1:
time: 95.7 us; the launch traced here: 95.1 us
  blocking collectives  46.9 us (49%)
  starting transfers between devices  13.5 us (14%)
  other arithmetic  12.3 us (13%)
  waiting for transfers between devices  11.7 us (12%)
  local copies, waits for them, and re-layouts  8.08 us (8%)
  between operations  1.82 us (2%)
    psum x2, blocking collectives, per_device(): cluster_total = lax.psum(lax.psum(partial_value, ('gy', 'gz')), 'gx')  22.6 us
    all_gather x1, blocking collectives, interface_z(): gathered = lax.all_gather(coeffs[None], 'gz', axis=0, tiled=True)  13.8 us
    ppermute x3, waiting for transfers between devices, padded(): after = lax.ppermute(first, axis, down)  10.3 us
    ppermute x3, starting transfers between devices, padded(): before = lax.ppermute(last, axis, up)  9.62 us
    all_gather x1, blocking collectives, interface_x(): gathered = lax.all_gather(coeffs[None], 'gx', axis=0, tiled=True)  8.61 us
    another operation x2, other arithmetic, per_device(): joined_outputs = jnp.stack([thermal_field, voxel_thermal_link])  6.1 us
    ppermute x3, starting transfers between devices, padded(): after = lax.ppermute(first, axis, down)  3.88 us
    slice x50, local copies, waits for them, and re-layouts, shifted(): lax.slice_in_dim(values, 0, length - offset, axis=axis)  2.41 us
  transfers between devices with their start and end apart: 6, of which 4 were waited for; matrix products, arithmetic and copies ran while one was open for 0% of the time, Pallas kernels for 0%

profile of v1, /device:TPU:0, one launch (start us, length us, event | category | flops | bytes accessed | tf_op | source)
XLA Modules:
  0.0 95.1 jit_solution(9688698769205649540)
XLA Ops:
  0.6 1.6 %fusion.115 = (f32[1]{0:T(128)}, f32[1]{0:T(128)}, f32[1]{0:T(128)}, f32[1]{0:T(128)}, f32[1]{0:T(128)}, /*index=5*/f32[1]{0:T(128)}, f32[1]{0:T(128)}, f32[1]{0:T(128)}) fusion(f32[8]{0:T(128)} %param.21), kind=kLoop, calls=%fused_computation.347 | loop fusion | bytes 64 | tf_op jit(solution)/shard_map/slice | solution.py:152
  2.3 6.0 %add_bitcast_fusion = f32[1,8,16,128]{3,2,1,0:T(8,128)S(1)} fusion(s32[8,16,128]{2,1,0:T(8,128)} %param.20, f32[]{:T(128)} %bitcast.8, f32[]{:T(128)} %bitcast.7, f32[]{:T(128)} %bitcast.6, f32[]{:T(128)} %bitcast.5, f32[]{:T(128)} %bitcast.4, f32[]{:T(128)} %bitcast.3, f32[]{:T(128)} %bitcast.2, f32[]{:T(128)} %bitcast.1), kind=kLoop, calls=%fused_computation.203 | loop fusion | flops 376832 | bytes 131104 | tf_op jit(solution)/shard_map/stack | solution.py:154
  8.4 4.8 %collective-permute-start = (f32[2,8,16,1]{3,2,1,0:T(8,128)S(1)}, f32[2,8,16,1]{3,2,1,0:T(8,128)S(1)}, u32[]{:S(2)}, u32[]{:S(2)}) collective-permute-start(f32[2,8,16,1]{3,2,1,0:T(8,128)S(1)} %get-tuple-element.1143), channel_id=1, source_target_pairs={{0,8},{8,16},{16,24},{1,9},{9,17},{17,25},{2,10},{10,18},{18,26},{... | collective-permute-start | bytes 3080 | tf_op jit(solution)/shard_map/ppermute | solution.py:22
  13.2 1.3 %collective-permute-start.1 = (f32[2,8,16,1]{3,2,1,0:T(8,128)S(1)}, f32[2,8,16,1]{3,2,1,0:T(8,128)S(1)}, u32[]{:S(2)}, u32[]{:S(2)}) collective-permute-start(f32[2,8,16,1]{3,2,1,0:T(8,128)S(1)} %get-tuple-element.1144), channel_id=1, source_target_pairs={{8,0},{16,8},{24,16},{9,1},{17,9},{25,17},{10,2},{18,10},{26,18},{... | collective-permute-start | bytes 3080 | tf_op jit(solution)/shard_map/ppermute | solution.py:23
  14.6 1.4 %collective-permute-done = f32[2,8,16,1]{3,2,1,0:T(8,128)S(1)} collective-permute-done((f32[2,8,16,1]{3,2,1,0:T(8,128)S(1)}, f32[2,8,16,1]{3,2,1,0:T(8,128)S(1)}, u32[]{:S(2)}, u32[]{:S(2)}) %collective-permute-start) | collective-permute-done | bytes 1056 | tf_op jit(solution)/shard_map/ppermute | solution.py:22
  16.0 4.8 %collective-permute-done.1 = f32[2,8,16,1]{3,2,1,0:T(8,128)S(1)} collective-permute-done((f32[2,8,16,1]{3,2,1,0:T(8,128)S(1)}, f32[2,8,16,1]{3,2,1,0:T(8,128)S(1)}, u32[]{:S(2)}, u32[]{:S(2)}) %collective-permute-start.1) | collective-permute-done | bytes 1056 | tf_op jit(solution)/shard_map/ppermute | solution.py:23
  20.7 0.2 pad_maximum_fusion.11
  20.9 1.3 %collective-permute-start.2 = (f32[2,8,1,130]{3,1,2,0:T(8,128)S(1)}, f32[2,8,1,130]{3,1,2,0:T(8,128)S(1)}, u32[]{:S(2)}, u32[]{:S(2)}) collective-permute-start(f32[2,8,1,130]{3,1,2,0:T(8,128)S(1)} %copy.710), channel_id=1, source_target_pairs={{0,4},{1,5},{2,6},{3,7},{8,12},{9,13},{10,14},{11,15},{16,20},{17,... | collective-permute-start | bytes 24968 | tf_op jit(solution)/shard_map/ppermute | solution.py:22
  22.2 1.3 %collective-permute-start.3 = (f32[2,8,1,130]{3,1,2,0:T(8,128)S(1)}, f32[2,8,1,130]{3,1,2,0:T(8,128)S(1)}, u32[]{:S(2)}, u32[]{:S(2)}) collective-permute-start(f32[2,8,1,130]{3,1,2,0:T(8,128)S(1)} %copy.711), channel_id=1, source_target_pairs={{4,0},{5,1},{6,2},{7,3},{12,8},{13,9},{14,10},{15,11},{20,16},{21,... | collective-permute-start | bytes 24968 | tf_op jit(solution)/shard_map/ppermute | solution.py:23
  23.6 1.7 %collective-permute-done.3 = f32[2,8,1,130]{3,1,2,0:T(8,128)S(1)} collective-permute-done((f32[2,8,1,130]{3,1,2,0:T(8,128)S(1)}, f32[2,8,1,130]{3,1,2,0:T(8,128)S(1)}, u32[]{:S(2)}, u32[]{:S(2)}) %collective-permute-start.3) | collective-permute-done | bytes 8352 | tf_op jit(solution)/shard_map/ppermute | solution.py:23
  25.4 3.5 %collective-permute-start.4 = (f32[2,1,18,130]{3,2,1,0:T(8,128)S(1)}, f32[2,1,18,130]{3,2,1,0:T(8,128)S(1)}, u32[]{:S(2)}, u32[]{:S(2)}) collective-permute-start(f32[2,1,18,130]{3,2,1,0:T(8,128)S(1)} %get-tuple-element.1066), channel_id=1, source_target_pairs={{0,1},{1,2},{2,3},{4,5},{5,6},{6,7},{8,9},{9,10},{10,11},{12,13},{... | collective-permute-start | bytes 56168 | tf_op jit(solution)/shard_map/ppermute | solution.py:22
  28.9 1.3 %collective-permute-start.5 = (f32[2,1,18,130]{3,2,1,0:T(8,128)S(1)}, f32[2,1,18,130]{3,2,1,0:T(8,128)S(1)}, u32[]{:S(2)}, u32[]{:S(2)}) collective-permute-start(f32[2,1,18,130]{3,2,1,0:T(8,128)S(1)} %get-tuple-element.1067), channel_id=1, source_target_pairs={{1,0},{2,1},{3,2},{5,4},{6,5},{7,6},{9,8},{10,9},{11,10},{13,12},{... | collective-permute-start | bytes 56168 | tf_op jit(solution)/shard_map/ppermute | solution.py:23
  30.3 0.7 copy-done.2
  31.1 3.8 %collective-permute-done.5 = f32[2,1,18,130]{3,2,1,0:T(8,128)S(1)} collective-permute-done((f32[2,1,18,130]{3,2,1,0:T(8,128)S(1)}, f32[2,1,18,130]{3,2,1,0:T(8,128)S(1)}, u32[]{:S(2)}, u32[]{:S(2)}) %collective-permute-start.5) | collective-permute-done | bytes 18752 | tf_op jit(solution)/shard_map/ppermute | solution.py:23
  34.9 0.2 pad_maximum_fusion
  35.8 0.8 copy-done.1
  36.7 0.2 fusion.14
  38.5 0.2 multiply_add_fusion.46
  39.2 0.2 multiply_add_fusion.44
  40.0 0.2 multiply_add_fusion.42
  40.8 0.2 multiply_add_fusion.40
  42.8 8.6 %all-gather = f32[24,8,16]{2,1,0:T(8,128)S(1)} all-gather(f32[6,8,16]{2,1,0:T(8,128)S(1)} %constant_dynamic-update-slice_fusion), channel_id=2, replica_groups=mesh['gx'=4,'gy'=2,'gz'=4] {'gx'}, dimensions={0}, use_global_device_ids=true | all-gather | bytes 15360 | tf_op jit(solution)/shard_map/all_gather | solution.py:60
  51.4 0.3 while.120
  53.0 1.8 %all-gather.1 = f32[12,8,128]{2,1,0:T(8,128)S(1)} all-gather(f32[6,8,128]{2,1,0:T(8,128)S(1)} %constant_dynamic-update-slice_fusion.6), channel_id=3, replica_groups=mesh['gx'=4,'gy'=2,'gz'=4] {'gy'}, dimensions={0}, use_global_device_ids=true | all-gather | bytes 73728 | tf_op jit(solution)/shard_map/all_gather | solution.py:65
  55.9 13.8 %all-gather.2 = f32[24,16,128]{2,1,0:T(8,128)S(1)} all-gather(f32[6,16,128]{2,1,0:T(8,128)S(1)} %constant_dynamic-update-slice_fusion.12), channel_id=4, replica_groups=mesh['gx'=4,'gy'=2,'gz'=4] {'gz'}, dimensions={0}, use_global_device_ids=true | all-gather | bytes 245760 | tf_op jit(solution)/shard_map/all_gather | solution.py:70
  69.8 0.3 while.124
  70.3 0.7 fusion.33
  71.2 0.2 convolution_bitcast_fusion.1
  71.4 13.7 %psum.14 = f32[64]{0:T(128)S(1)} all-reduce(f32[64]{0:T(128)S(1)} %convolution_bitcast_fusion.1), channel_id=1, replica_groups=mesh['gx'=4,'gy'=2,'gz'=4] {'gy','gz'}, use_global_device_ids=true, to_apply=%region_14.15 | all-reduce | flops 64 | bytes 512 | tf_op jit(solution)/shard_map/psum | solution.py:192
  85.1 8.9 %psum.15 = f32[64]{0:T(128)S(1)} all-reduce(f32[64]{0:T(128)S(1)} %psum.14), channel_id=1, replica_groups=mesh['gx'=4,'gy'=2,'gz'=4] {'gx'}, use_global_device_ids=true, to_apply=%region_15.16 | all-reduce | flops 64 | bytes 512 | tf_op jit(solution)/shard_map/psum | solution.py:192
  94.0 0.2 convolution_bitcast_fusion
  94.5 0.6 broadcast_add_fusion
  (230 shorter events, 9.2 us)
Async XLA Ops:
  2.2 6.0 %copy-start = (f32[8,16,128]{2,1,0:T(8,128)S(1)}, f32[8,16,128]{2,1,0:T(8,128)}, u32[]{:S(2)}) copy-start(f32[8,16,128]{2,1,0:T(8,128)} %param.18) | copy-start | bytes 196612
  8.4 7.6 %collective-permute-start = (f32[2,8,16,1]{3,2,1,0:T(8,128)S(1)}, f32[2,8,16,1]{3,2,1,0:T(8,128)S(1)}, u32[]{:S(2)}, u32[]{:S(2)}) collective-permute-start(f32[2,8,16,1]{3,2,1,0:T(8,128)S(1)} %get-tuple-element.1143), channel_id=1, source_target_pairs={{0,8},{8,16},{16,24},{1,9},{9,17},{17,25},{2,10},{10,18},{18,26},{... | collective-permute-start | bytes 3080 | tf_op jit(solution)/shard_map/ppermute | solution.py:22
  13.2 7.5 %collective-permute-start.1 = (f32[2,8,16,1]{3,2,1,0:T(8,128)S(1)}, f32[2,8,16,1]{3,2,1,0:T(8,128)S(1)}, u32[]{:S(2)}, u32[]{:S(2)}) collective-permute-start(f32[2,8,16,1]{3,2,1,0:T(8,128)S(1)} %get-tuple-element.1144), channel_id=1, source_target_pairs={{8,0},{16,8},{24,16},{9,1},{17,9},{25,17},{10,2},{18,10},{26,18},{... | collective-permute-start | bytes 3080 | tf_op jit(solution)/shard_map/ppermute | solution.py:23
  20.9 2.6 %collective-permute-start.2 = (f32[2,8,1,130]{3,1,2,0:T(8,128)S(1)}, f32[2,8,1,130]{3,1,2,0:T(8,128)S(1)}, u32[]{:S(2)}, u32[]{:S(2)}) collective-permute-start(f32[2,8,1,130]{3,1,2,0:T(8,128)S(1)} %copy.710), channel_id=1, source_target_pairs={{0,4},{1,5},{2,6},{3,7},{8,12},{9,13},{10,14},{11,15},{16,20},{17,... | collective-permute-start | bytes 24968 | tf_op jit(solution)/shard_map/ppermute | solution.py:22
  22.2 3.1 %collective-permute-start.3 = (f32[2,8,1,130]{3,1,2,0:T(8,128)S(1)}, f32[2,8,1,130]{3,1,2,0:T(8,128)S(1)}, u32[]{:S(2)}, u32[]{:S(2)}) collective-permute-start(f32[2,8,1,130]{3,1,2,0:T(8,128)S(1)} %copy.711), channel_id=1, source_target_pairs={{4,0},{5,1},{6,2},{7,3},{12,8},{13,9},{14,10},{15,11},{20,16},{21,... | collective-permute-start | bytes 24968 | tf_op jit(solution)/shard_map/ppermute | solution.py:23
  25.4 5.7 %collective-permute-start.4 = (f32[2,1,18,130]{3,2,1,0:T(8,128)S(1)}, f32[2,1,18,130]{3,2,1,0:T(8,128)S(1)}, u32[]{:S(2)}, u32[]{:S(2)}) collective-permute-start(f32[2,1,18,130]{3,2,1,0:T(8,128)S(1)} %get-tuple-element.1066), channel_id=1, source_target_pairs={{0,1},{1,2},{2,3},{4,5},{5,6},{6,7},{8,9},{9,10},{10,11},{12,13},{... | collective-permute-start | bytes 56168 | tf_op jit(solution)/shard_map/ppermute | solution.py:22
  28.9 6.0 %collective-permute-start.5 = (f32[2,1,18,130]{3,2,1,0:T(8,128)S(1)}, f32[2,1,18,130]{3,2,1,0:T(8,128)S(1)}, u32[]{:S(2)}, u32[]{:S(2)}) collective-permute-start(f32[2,1,18,130]{3,2,1,0:T(8,128)S(1)} %get-tuple-element.1067), channel_id=1, source_target_pairs={{1,0},{2,1},{3,2},{5,4},{6,5},{7,6},{9,8},{10,9},{11,10},{13,12},{... | collective-permute-start | bytes 56168 | tf_op jit(solution)/shard_map/ppermute | solution.py:23
  30.3 0.7 copy-start.2
  35.8 0.8 copy-start.1
  85.1 8.9 %copy-start.3 = (f32[64]{0:T(128)S(1)}, f32[64]{0:T(128)}, u32[]{:S(2)}) copy-start(f32[64]{0:T(128)} %param.23) | copy-start | bytes 772
